TPU v7x, 32 devices: a whole 2x2x4 slice. The times are simulated.
32 devices in a mesh: seg: 4 (over y, x), sec: 8 (over z, core).
Axes of the slice: x: 2, y: 2, z: 4, core: 2. Of those that a mesh axis runs over, the one named last changes fastest.
Arguments:
- left_env: bfloat16 [4, 8, 13, 512, 512], P('seg', 'sec'), may hold values from -0.25 to 0.25
- right_env: bfloat16 [4, 8, 13, 512, 512], P('seg', 'sec'), may hold values from -0.25 to 0.25
- left_block: bfloat16 [4, 8, 512, 512], P('seg', 'sec'), may hold values from -8 to 8
- right_block: bfloat16 [4, 8, 512, 512], P('seg', 'sec'), may hold values from -0.25 to 0.25
- inv_sv: bfloat16 [4, 8, 512], P('seg', 'sec'), may hold values from 0.5 to 2
- precond: float32 [4, 8, 512, 512], P('seg', 'sec'), may hold values from 1 to 4
- sector_dims: int32 [4, 8, 2], P('seg', 'sec'), may hold values from 128 to 512, as said below
- channel_charge: int32 [13], replicated, may hold values from -1 to 1
Outputs:
- next_vector: bfloat16 [4, 8, 512, 512], P('seg', 'sec')
- last_image: float32 [4, 8, 512, 512], P('seg', 'sec')
- projected: float32 [4, 4, 4], P('seg')
Inputs may be any that keep to these rules, and one draw needn't show every extreme that they name: `sector_dims`: in every segment some sector has left bond dimension 512 and some sector has right bond dimension 512.
All inputs are finite; a program needn't handle non-finite values.
Results may differ from a plain program's by a relative error of at most 0.024.
Values may be sent and summed in bfloat16 or wider, within the bound.
A program may use at most 64 MiB of HBM per device.

v0:
```python
import jax
import jax.numpy as jnp
from jax import lax
from jax.sharding import PartitionSpec as P

MATVECS = 4


def shifted(block, axis, distance):
    devices = range(lax.axis_size(axis))
    route = [((i - distance) % len(devices), i) for i in devices]
    return lax.ppermute(block, axis, route)


def shifted_2(x, axis, by):
    count = lax.axis_size(axis)
    pairs = [(i, i + by) for i in range(count) if 0 <= i + by < count]
    return lax.ppermute(x, axis, pairs)


def per_device(
    left_env, right_env, left_block, right_block, inv_sv, precond, sector_dims, channel_charge
):
    eps = 1e-06
    width = left_block.shape[-1]
    count = lax.axis_size("sec") * width * width
    lenv = left_env[0, 0]
    renv = right_env[0, 0]
    dims = sector_dims[0, 0]
    scale_inv = precond[0, 0]
    index = jnp.arange(width, dtype=jnp.int32)
    mask = ((index[:, None] < dims[0]) & (index[None, :] < dims[1])).astype(jnp.float32)
    neighbour_block, neighbour_inv = shifted((right_block[0, 0], inv_sv[0, 0]), "seg", -1)
    scaled = (
        left_block[0, 0].astype(jnp.float32) * neighbour_inv.astype(jnp.float32)[None, :]
    ).astype(jnp.bfloat16)
    guess = jnp.dot(scaled, neighbour_block, preferred_element_type=jnp.float32) * mask

    def local_dot(first, second):
        return jnp.sum(first * second) / count

    (guess_sq,) = lax.psum((local_dot(guess, guess),), "sec")
    first = (guess * lax.rsqrt(guess_sq + eps)).astype(jnp.bfloat16)
    select = (channel_charge[:, None] == jnp.array([-1, 0, 1], dtype=jnp.int32)[None, :]).astype(
        jnp.float32
    )
    basis = [first]
    basis_float = [first.astype(jnp.float32)]
    gram_rows = []
    columns = []
    image = None
    for step in range(MATVECS):
        current = basis[step]
        left_x = jnp.einsum(
            "wab,bc->wac", lenv, current, preferred_element_type=jnp.float32
        ).astype(jnp.bfloat16)
        terms = jnp.einsum("wac,wdc->wad", left_x, renv, preferred_element_type=jnp.float32)
        to_lower = jnp.sum(terms * select[:, 0, None, None], axis=0)
        stay = jnp.sum(terms * select[:, 1, None, None], axis=0)
        to_upper = jnp.sum(terms * select[:, 2, None, None], axis=0)
        from_lower = shifted_2(to_upper.astype(jnp.bfloat16), "sec", 1).astype(to_upper.dtype)
        from_upper = shifted_2(to_lower.astype(jnp.bfloat16), "sec", -1).astype(to_lower.dtype)
        image = (stay + from_lower + from_upper) * mask
        gathered = lax.psum(
            tuple((local_dot(basis_float[j], image) for j in range(step + 1)))
            + tuple((local_dot(basis_float[j], basis_float[step]) for j in range(step + 1))),
            "sec",
        )
        column = list(gathered[: step + 1])
        gram_rows.append(list(gathered[step + 1 :]))
        theta = column[step]
        columns.append(
            jnp.stack(column + [jnp.zeros((), jnp.float32) for j in range(MATVECS - step - 1)])
        )
        correction = (image - theta * basis_float[step]) / scale_inv
        gathered = lax.psum(
            tuple((local_dot(basis_float[j], correction) for j in range(step + 1)))
            + (local_dot(correction, correction),),
            "sec",
        )
        weights = list(gathered[: step + 1])
        total_sq = gathered[step + 1]
        for i in range(step + 1):
            total_sq = total_sq - 2.0 * weights[i] * weights[i]
            for j in range(step + 1):
                entry = gram_rows[max(i, j)][min(i, j)]
                total_sq = total_sq + weights[i] * weights[j] * entry
        remain = correction
        for j in range(step + 1):
            remain = remain - weights[j] * basis_float[j]
        following = (remain * lax.rsqrt(total_sq + eps)).astype(jnp.bfloat16)
        basis.append(following)
        basis_float.append(following.astype(jnp.float32))
    projected = jnp.stack(columns, axis=1)
    return (basis[-1][None, None], image[None, None], projected[None])


def solution(mesh):
    in_specs = (
        P("seg", "sec", None, None, None),
        P("seg", "sec", None, None, None),
        P("seg", "sec", None, None),
        P("seg", "sec", None, None),
        P("seg", "sec", None),
        P("seg", "sec", None, None),
        P("seg", "sec", None),
        P(),
    )
    out_specs = (P("seg", "sec", None, None), P("seg", "sec", None, None), P("seg", None, None))
    return jax.shard_map(
        per_device, mesh=mesh, in_specs=in_specs, out_specs=out_specs, check_vma=False
    )
```

profile of v0, /device:TPU:0, one launch (start us, length us, event | category | flops | bytes accessed | tf_op | source)
XLA Modules:
  0.0 385.5 jit_solution(2211952548859648006)
XLA Ops:
  0.6 4.0 %collective-permute-start.1 = (bf16[512,512]{1,0:T(8,128)(2,1)}, bf16[512,512]{1,0:T(8,128)(2,1)S(1)}, u32[]{:S(2)}, u32[]{:S(2)}) collective-permute-start(bf16[512,512]{1,0:T(8,128)(2,1)} %bitcast.145), channel_id=1, source_target_pairs={{8,0},{16,8},{24,16},{0,24},{9,1},{17,9},{25,17},{1,25},{10,2},{18... | collective-permute-start | bytes 1572872 | tf_op jit(solution)/shard_map/ppermute | solution.py:12
  9.2 6.9 %collective-permute-done = bf16[512]{0:T(512)(128)(2,1)S(1)} collective-permute-done((bf16[512]{0:T(512)(128)(2,1)S(1)}, bf16[512]{0:T(512)(128)(2,1)S(1)}, u32[]{:S(2)}, u32[]{:S(2)}) %collective-permute-start) | collective-permute-done | bytes 1056 | tf_op jit(solution)/shard_map/ppermute | solution.py:12
  16.1 2.2 multiply_reduce_fusion.16
  19.0 16.3 %psum.245 = f32[]{:T(128)} all-reduce(f32[]{:T(128)S(6)} %div.117), channel_id=1, replica_groups=mesh['seg'=4,'sec'=8] {'sec'}, use_global_device_ids=true, to_apply=%region_1.0 | all-reduce | flops 1 | bytes 8 | tf_op jit(solution)/shard_map/psum | solution.py:42
  36.0 14.6 %multiply_reduce_fusion.10 = (bf16[512,512]{1,0:T(8,128)(2,1)}, bf16[512,512]{1,0:T(8,128)(2,1)}, f32[512,512]{1,0:T(8,128)S(1)}) fusion(f32[13]{0:T(128)S(1)} %get-tuple-element.87, f32[13]{0:T(128)S(1)} %get-tuple-element.86, f32[13]{0:T(128)S(1)} %get-tuple-element.85, bf16[1,1,13,512,512]{4,3,2,1,0:T(8,128)(2,1)} %param.10, ...), kind=kOutput, calls=%fused_computation.10 | convolution fusion | flops 7002914816 | bytes 16777376 | tf_op jit(solution)/shard_map/wac,wdc->wad/dot_general | solution.py:57
  53.6 2.3 collective-permute-done.3
  58.5 19.5 %psum.246 = f32[]{:T(128)} all-reduce(f32[]{:T(128)S(6)} %div.118), channel_id=1, replica_groups=mesh['seg'=4,'sec'=8] {'sec'}, use_global_device_ids=true, to_apply=%region_6.0 | all-reduce | flops 1 | bytes 8 | tf_op jit(solution)/shard_map/psum | solution.py:64
  78.0 4.1 %fusion.71 = (f32[]{:T(128)}, f32[]{:T(128)}, f32[]{:T(128)}, f32[512,512]{1,0:T(8,128)}) fusion(f32[1,1,512,512]{3,2,1,0:T(8,128)S(1)} %copy-done, f32[]{:T(128)} %psum.246, bf16[512,512]{1,0:T(8,128)(2,1)} %copy-done.2, f32[512,512]{1,0:T(8,128)S(1)} %get-tuple-element.14, bf16[512,512]{1,0:T(8,128)(2,1)} %copy-done.1, ...), kind=kLoop, calls=%fused_computation.120 | loop fusion | flops 4718589 | bytes 5243924 | tf_op jit(solution)/shard_map/reduce_sum | solution.py:40
  83.9 14.4 %all-reduce.3 = (f32[]{:T(128)}, f32[]{:T(128)}, f32[]{:T(128)}) all-reduce(f32[]{:T(128)S(6)} %div.121, f32[]{:T(128)S(6)} %div.120, f32[]{:T(128)S(6)} %div.122), channel_id=1, replica_groups=mesh['seg'=4,'sec'=8] {'sec'}, use_global_device_ids=true, to_apply=%region_10.0 | all-reduce | flops 3 | bytes 24 | tf_op jit(solution)/shard_map/psum | solution.py:76
  102.4 2.2 fusion.74
  104.5 14.8 %multiply_reduce_fusion.7 = (bf16[512,512]{1,0:T(8,128)(2,1)}, bf16[512,512]{1,0:T(8,128)(2,1)}, f32[512,512]{1,0:T(8,128)}) fusion(f32[13]{0:T(128)S(1)} %get-tuple-element.87, f32[13]{0:T(128)S(1)} %get-tuple-element.86, f32[13]{0:T(128)S(1)} %get-tuple-element.85, bf16[1,1,13,512,512]{4,3,2,1,0:T(8,128)(2,1)} %param.10, ...), kind=kOutput, calls=%fused_computation.7 | convolution fusion | flops 7002390528 | bytes 16253084 | tf_op jit(solution)/shard_map/wac,wdc->wad/dot_general | solution.py:57
  122.9 2.3 collective-permute-done.5
  125.2 3.4 fusion.85
  129.3 20.8 %psum.250 = f32[]{:T(128)} all-reduce(f32[]{:T(128)S(6)} %div.123), channel_id=1, replica_groups=mesh['seg'=4,'sec'=8] {'sec'}, use_global_device_ids=true, to_apply=%region_17.0 | all-reduce | flops 1 | bytes 8 | tf_op jit(solution)/shard_map/psum | solution.py:64
  150.1 3.9 %fusion.55 = (f32[]{:T(128)}, f32[]{:T(128)}, f32[]{:T(128)}, f32[512,512]{1,0:T(8,128)}) fusion(bf16[512,512]{1,0:T(8,128)(2,1)S(1)} %fusion.74, f32[1,1,512,512]{3,2,1,0:T(8,128)S(1)} %copy-done, f32[512,512]{1,0:T(8,128)} %get-tuple-element.83, f32[]{:T(128)} %psum.250, f32[512,512]{1,0:T(8,128)S(1)} %get-tuple-element.93, f32[]{:T(128)S(6)} %rsqrt.15), kind=kLoop, calls=%fused_computation.104 | loop fusion | flops 3407869 | bytes 4718612 | tf_op jit(solution)/shard_map/reduce_sum | solution.py:40
  157.0 14.4 %all-reduce.2 = (f32[]{:T(128)}, f32[]{:T(128)}, f32[]{:T(128)}, f32[]{:T(128)}, f32[]{:T(128)}) all-reduce(f32[]{:T(128)S(6)} %div.127, f32[]{:T(128)S(6)} %div.125, f32[]{:T(128)S(6)} %div.126, f32[]{:T(128)S(6)} %div.128, f32[]{:T(128)S(6)} %div.129), channel_id=1, replica_groups=mesh['seg'=4,'sec'=8] {'sec'}, use_global_device_ids=true, to_apply=%region_23.0 | all-reduce | flops 5 | bytes 40 | tf_op jit(solution)/shard_map/psum | solution.py:76
  180.1 2.8 fusion.58
  182.9 14.8 %multiply_reduce_fusion.4 = (bf16[512,512]{1,0:T(8,128)(2,1)}, bf16[512,512]{1,0:T(8,128)(2,1)}, f32[512,512]{1,0:T(8,128)}) fusion(f32[13]{0:T(128)S(1)} %get-tuple-element.87, f32[13]{0:T(128)S(1)} %get-tuple-element.86, f32[13]{0:T(128)S(1)} %get-tuple-element.85, bf16[1,1,13,512,512]{4,3,2,1,0:T(8,128)(2,1)} %param.10, ...), kind=kOutput, calls=%fused_computation.4 | convolution fusion | flops 7002390528 | bytes 16253084 | tf_op jit(solution)/shard_map/wac,wdc->wad/dot_general | solution.py:57
  201.2 2.3 collective-permute-done.7
  203.5 3.7 fusion.86
  207.9 20.8 %psum.256 = f32[]{:T(128)} all-reduce(f32[]{:T(128)S(6)} %div.130), channel_id=1, replica_groups=mesh['seg'=4,'sec'=8] {'sec'}, use_global_device_ids=true, to_apply=%region_32.0 | all-reduce | flops 1 | bytes 8 | tf_op jit(solution)/shard_map/psum | solution.py:64
  228.7 4.0 %fusion.43 = (f32[]{:T(128)}, f32[]{:T(128)}, f32[]{:T(128)}, f32[]{:T(128)}, f32[512,512]{1,0:T(8,128)}) fusion(bf16[512,512]{1,0:T(8,128)(2,1)S(1)} %fusion.58, bf16[512,512]{1,0:T(8,128)(2,1)S(1)} %fusion.74, f32[1,1,512,512]{3,2,1,0:T(8,128)S(1)} %copy-done, f32[512,512]{1,0:T(8,128)} %get-tuple-element.81, f32[]{:T(128)} %psum.256, ...), kind=kLoop, calls=%fused_computation.92 | loop fusion | flops 4194300 | bytes 5242904 | tf_op jit(solution)/shard_map/reduce_sum | solution.py:40
  237.2 14.4 %all-reduce.1 = (f32[]{:T(128)}, f32[]{:T(128)}, f32[]{:T(128)}, f32[]{:T(128)}, f32[]{:T(128)}, /*index=5*/f32[]{:T(128)}, f32[]{:T(128)}) all-reduce(f32[]{:T(128)S(6)} %div.135, f32[]{:T(128)S(6)} %div.132, f32[]{:T(128)S(6)} %div.133, f32[]{:T(128)S(6)} %div.134, f32[]{:T(128)S(6)} %div.136, ...), channel_id=1, replica_groups=mesh['seg'=4,'sec'=8] {'sec'}, use_global_device_ids=true, to_apply=%region_40.0 | all-reduce | flops 7 | bytes 56 | tf_op jit(solution)/shard_map/psum | solution.py:76
  267.5 4.3 %fusion.46 = bf16[512,512]{1,0:T(8,128)(2,1)} fusion(bf16[512,512]{1,0:T(8,128)(2,1)S(1)} %fusion.58, bf16[512,512]{1,0:T(8,128)(2,1)S(1)} %fusion.74, f32[512,512]{1,0:T(8,128)} %get-tuple-element.80, f32[]{:T(128)S(6)} %rsqrt.18, f32[]{:T(128)} %get-tuple-element.66, f32[]{:T(128)} %get-tuple-element.65, f32[]{:T(128)} %get-tuple-element.64, ...), kind=kLoop, calls=%fused_computation.95 | loop fusion | flops 3407872 | bytes 3670036 | tf_op jit(solution)/shard_map/convert_element_type | solution.py:91
  271.8 14.9 %multiply_reduce_fusion.1 = (bf16[512,512]{1,0:T(8,128)(2,1)}, bf16[512,512]{1,0:T(8,128)(2,1)}, f32[512,512]{1,0:T(8,128)}) fusion(f32[13]{0:T(128)S(1)} %get-tuple-element.87, f32[13]{0:T(128)S(1)} %get-tuple-element.86, f32[13]{0:T(128)S(1)} %get-tuple-element.85, bf16[1,1,13,512,512]{4,3,2,1,0:T(8,128)(2,1)} %param.10, ...), kind=kOutput, calls=%fused_computation.1 | convolution fusion | flops 7002390528 | bytes 16253084 | tf_op jit(solution)/shard_map/wac,wdc->wad/dot_general | solution.py:57
  286.7 2.6 collective-permute-start.8
  293.4 4.3 %fusion.87 = (f32[]{:T(128)}, f32[]{:T(128)}, f32[]{:T(128)}, f32[]{:T(128)}, f32[]{:T(128)}, /*index=5*/f32[]{:T(128)}, f32[]{:T(128)}, f32[]{:T(128)}, f32[512,512]{1,0:T(8,128)}) fusion(bf16[512,512]{1,0:T(8,128)(2,1)S(1)} %fusion.58, bf16[512,512]{1,0:T(8,128)(2,1)S(1)} %fusion.74, bf16[512,512]{1,0:T(8,128)(2,1)} %fusion.46, ...), kind=kLoop, calls=%fused_computation.136 | loop fusion | flops 7340024 | bytes 5768228 | tf_op jit(solution)/shard_map/reduce_sum | solution.py:40
  299.0 20.1 %psum.264 = f32[]{:T(128)} all-reduce(f32[]{:T(128)S(6)} %div.139), channel_id=1, replica_groups=mesh['seg'=4,'sec'=8] {'sec'}, use_global_device_ids=true, to_apply=%region_51.0 | all-reduce | flops 1 | bytes 8 | tf_op jit(solution)/shard_map/psum | solution.py:64
  319.1 4.4 %fusion.35 = (f32[]{:T(128)}, f32[]{:T(128)}, f32[]{:T(128)}, f32[]{:T(128)}, f32[]{:T(128)}, /*index=5*/f32[512,512]{1,0:T(8,128)}) fusion(bf16[512,512]{1,0:T(8,128)(2,1)} %fusion.46, bf16[512,512]{1,0:T(8,128)(2,1)S(1)} %fusion.58, bf16[512,512]{1,0:T(8,128)(2,1)S(1)} %fusion.74, f32[1,1,512,512]{3,2,1,0:T(8,128)S(1)} %copy-done, ...), kind=kLoop, calls=%fused_computation.84 | loop fusion | flops 4980731 | bytes 5767196 | tf_op jit(solution)/shard_map/reduce_sum | solution.py:40
  330.9 17.8 %all-reduce = (f32[]{:T(128)}, f32[]{:T(128)}, f32[]{:T(128)}, f32[]{:T(128)}, f32[]{:T(128)}, /*index=5*/f32[]{:T(128)}, f32[]{:T(128)}, f32[]{:T(128)}, f32[]{...) all-reduce(f32[]{:T(128)S(6)} %div.145, ...), channel_id=1, replica_groups=mesh['seg'=4,'sec'=8] {'sec'}, use_global_device_ids=true, to_apply=%region_61.0 | all-reduce | flops 15 | bytes 120 | tf_op jit(solution)/shard_map/psum | solution.py:76
  367.7 2.6 maximum_bitcast_fusion.1
  380.3 5.2 %fusion.100 = bf16[1,1,512,512]{3,2,1,0:T(8,128)(2,1)} fusion(f32[]{:T(128)S(6)} %rsqrt.19, bf16[512,512]{1,0:T(8,128)(2,1)} %fusion.46, f32[]{:T(128)} %get-tuple-element.52, bf16[512,512]{1,0:T(8,128)(2,1)S(1)} %fusion.58, f32[]{:T(128)} %get-tuple-element.51, bf16[512,512]{1,0:T(8,128)(2,1)S(1)} %fusion.74, f32[]{:T(128)} %get-tuple-element.50, ...), kind=kLoop, calls=%fused_computation.151 | loop fusion | flops 4194304 | bytes 4194328 | tf_op jit(solution)/shard_map/broadcast_in_dim | solution.py:95
  (32 shorter events, 24.0 us)
Async XLA Ops:
  0.6 15.5 %collective-permute-start.1 = (bf16[512,512]{1,0:T(8,128)(2,1)}, bf16[512,512]{1,0:T(8,128)(2,1)S(1)}, u32[]{:S(2)}, u32[]{:S(2)}) collective-permute-start(bf16[512,512]{1,0:T(8,128)(2,1)} %bitcast.145), channel_id=1, source_target_pairs={{8,0},{16,8},{24,16},{0,24},{9,1},{17,9},{25,17},{1,25},{10,2},{18... | collective-permute-start | bytes 1572872 | tf_op jit(solution)/shard_map/ppermute | solution.py:12
  5.3 10.8 %collective-permute-start = (bf16[512]{0:T(512)(128)(2,1)S(1)}, bf16[512]{0:T(512)(128)(2,1)S(1)}, u32[]{:S(2)}, u32[]{:S(2)}) collective-permute-start(bf16[512]{0:T(512)(128)(2,1)S(1)} %reduce), channel_id=1, source_target_pairs={{8,0},{16,8},{24,16},{0,24},{9,1},{17,9},{25,17},{1,25},{10,2},{18... | collective-permute-start | bytes 3080 | tf_op jit(solution)/shard_map/ppermute | solution.py:12
  36.0 42.0 %copy-start = (f32[1,1,512,512]{3,2,1,0:T(8,128)S(1)}, f32[1,1,512,512]{3,2,1,0:T(8,128)}, u32[]{:S(2)}) copy-start(f32[1,1,512,512]{3,2,1,0:T(8,128)} %param.14) | copy-start | bytes 3145732
  50.6 3.0 collective-permute-start.2
  51.9 4.0 %collective-permute-start.3 = (bf16[512,512]{1,0:T(8,128)(2,1)}, bf16[512,512]{1,0:T(8,128)(2,1)S(1)}, u32[]{:S(2)}, u32[]{:S(2)}) collective-permute-start(bf16[512,512]{1,0:T(8,128)(2,1)} %get-tuple-element.13), channel_id=1, source_target_pairs={{1,0},{2,1},{3,2},{4,3},{5,4},{6,5},{7,6},{9,8},{10,9},{11,10},{12... | collective-permute-start | bytes 1572872 | tf_op jit(solution)/shard_map/ppermute | solution.py:18
  53.6 2.3 copy-start.1
  55.9 0.8 copy-start.2
  119.4 3.5 collective-permute-start.4
  121.2 4.0 %collective-permute-start.5 = (bf16[512,512]{1,0:T(8,128)(2,1)}, bf16[512,512]{1,0:T(8,128)(2,1)S(1)}, u32[]{:S(2)}, u32[]{:S(2)}) collective-permute-start(bf16[512,512]{1,0:T(8,128)(2,1)} %get-tuple-element.10), channel_id=1, source_target_pairs={{1,0},{2,1},{3,2},{4,3},{5,4},{6,5},{7,6},{9,8},{10,9},{11,10},{12... | collective-permute-start | bytes 1572872 | tf_op jit(solution)/shard_map/ppermute | solution.py:18
  197.7 3.5 collective-permute-start.6
  199.5 4.0 %collective-permute-start.7 = (bf16[512,512]{1,0:T(8,128)(2,1)}, bf16[512,512]{1,0:T(8,128)(2,1)S(1)}, u32[]{:S(2)}, u32[]{:S(2)}) collective-permute-start(bf16[512,512]{1,0:T(8,128)(2,1)} %get-tuple-element.7), channel_id=1, source_target_pairs={{1,0},{2,1},{3,2},{4,3},{5,4},{6,5},{7,6},{9,8},{10,9},{11,10},{12... | collective-permute-start | bytes 1572872 | tf_op jit(solution)/shard_map/ppermute | solution.py:18
  286.7 5.2 %collective-permute-start.8 = (bf16[512,512]{1,0:T(8,128)(2,1)}, bf16[512,512]{1,0:T(8,128)(2,1)}, u32[]{:S(2)}, u32[]{:S(2)}) collective-permute-start(bf16[512,512]{1,0:T(8,128)(2,1)} %get-tuple-element.3), channel_id=1, source_target_pairs={{0,1},{1,2},{2,3},{3,4},{4,5},{5,6},{6,7},{8,9},{9,10},{10,11},{11... | collective-permute-start | bytes 1572872 | tf_op jit(solution)/shard_map/ppermute | solution.py:18
  289.3 4.1 %collective-permute-start.9 = (bf16[512,512]{1,0:T(8,128)(2,1)}, bf16[512,512]{1,0:T(8,128)(2,1)}, u32[]{:S(2)}, u32[]{:S(2)}) collective-permute-start(bf16[512,512]{1,0:T(8,128)(2,1)} %get-tuple-element.4), channel_id=1, source_target_pairs={{1,0},{2,1},{3,2},{4,3},{5,4},{6,5},{7,6},{9,8},{10,9},{11,10},{12... | collective-permute-start | bytes 1572872 | tf_op jit(solution)/shard_map/ppermute | solution.py:18
where the time goes:
time: 388 us; the launch traced here: 386 us
  blocking collectives  158 us (41%)
  between operations  76.6 us (20%)
  matrix products  61.3 us (16%)
  other arithmetic  52.6 us (14%)
  starting transfers between devices  17.3 us (4%)
  waiting for transfers between devices  16.5 us (4%)
    psum x4, blocking collectives, per_device(): lax.psum(tuple((local_dot(basis_float[j], image) for j in range(step + 1)...  81.1 us
    psum x4, blocking collectives, per_device(): lax.psum(tuple((local_dot(basis_float[j], correction) for j in range(step...  61 us
    dot_general x4, matrix products, per_device(): jnp.einsum('wac,wdc->wad', left_x, renv, preferred_element_type=jnp.float32)  59.1 us
    reduce_sum x8, other arithmetic, local_dot(): return jnp.sum(first * second) / count  28.9 us
    psum x1, blocking collectives, per_device(): guess_sq, = lax.psum((local_dot(guess, guess),), 'sec')  16.3 us
    ppermute x8, starting transfers between devices, shifted_2(): return lax.ppermute(x, axis, pairs)  12.7 us
    ppermute x8, waiting for transfers between devices, shifted_2(): return lax.ppermute(x, axis, pairs)  9.67 us
    convert_element_type x3, other arithmetic, per_device(): following = (remain * lax.rsqrt(total_sq + eps)).astype(jnp.bfloat16)  9.27 us
  transfers between devices with their start and end apart: 10, of which 8 were waited for; matrix products, arithmetic and copies ran while one was open for 1% of the time, Pallas kernels for 0%

commit v1 on v0

v1 whole, which is shorter than its diff:
```python
import functools

import jax
import jax.numpy as jnp
from jax import lax
from jax.experimental import pallas as pl
from jax.experimental.pallas import tpu as pltpu
from jax.sharding import PartitionSpec as P

MATVECS = 4
EPS = 1e-06
ROWS = 128
CHUNK = 32
MESH = pl.DeviceIdType.MESH


def fold(values):
    rows, columns = values.shape
    block = jnp.sum(values.reshape(rows // 8, 8, columns), axis=0)
    total = block[:, :128]
    for at in range(128, columns, 128):
        total = total + block[:, at : at + 128]
    return total


def kernel(
    segs, secs,
    charge_ref, dims_ref, left_hbm, right_hbm, block_ref, other_hbm, inv_ref, precond_ref,
    next_ref, image_ref, projected_ref,
    left_ref, right_ref, nb_ref, ninv_ref, scaled_ref, pinv_ref, basis_ref, lx_ref, prefix_ref,
    stay_ref, up_out, low_out, up_in, low_in, slots_ref, rows_ref, gram_ref, proj_ref, order_ref,
    load_sem, guess_send, guess_recv, halo_send, halo_recv, sum_send, sum_recv,
):
    channels, width, _ = left_ref.shape
    tiles = width // ROWS
    count = secs * width * width
    f32, bf16 = jnp.float32, jnp.bfloat16
    seg, sec = lax.axis_index("seg"), lax.axis_index("sec")
    seg_before = lax.rem(seg + segs - 1, segs)
    seg_after = lax.rem(seg + 1, segs)

    load_left = pltpu.make_async_copy(left_hbm, left_ref, load_sem.at[0])
    load_right = pltpu.make_async_copy(right_hbm, right_ref, load_sem.at[1])
    load_left.start()
    load_right.start()

    barrier = pltpu.get_barrier_semaphore()
    pl.semaphore_signal(barrier, inc=1, device_id=(seg_before, sec), device_id_type=MESH)
    pl.semaphore_signal(barrier, inc=1, device_id=(seg_after, sec), device_id_type=MESH)
    for offset in range(1, secs):
        peer = lax.rem(sec + offset, secs)
        pl.semaphore_signal(barrier, inc=1, device_id=(seg, peer), device_id_type=MESH)
    pl.semaphore_wait(barrier, secs + 1)

    def remote(src, dst, send, recv, device):
        return pltpu.make_async_remote_copy(
            src_ref=src, dst_ref=dst, send_sem=send, recv_sem=recv,
            device_id=device, device_id_type=MESH,
        )

    send_inv = remote(
        inv_ref, ninv_ref, guess_send.at[0], guess_recv.at[0], (seg_before, sec)
    )
    send_block = remote(
        other_hbm, nb_ref, guess_send.at[1], guess_recv.at[1], (seg_before, sec)
    )
    send_inv.start()
    send_block.start()

    keys = []
    for w in range(channels):
        q = charge_ref[w]
        keys.append(jnp.where(q == 1, 0, jnp.where(q == -1, 1, 2)))
    raising = jnp.int32(0)
    moving = jnp.int32(0)
    for w in range(channels):
        raising = raising + jnp.where(keys[w] == 0, 1, 0)
        moving = moving + jnp.where(keys[w] <= 1, 1, 0)
    places = []
    for w in range(channels):
        place = jnp.int32(0)
        for v in range(channels):
            if v < w:
                place = place + jnp.where(keys[v] <= keys[w], 1, 0)
            elif v > w:
                place = place + jnp.where(keys[v] < keys[w], 1, 0)
        places.append(place)
    for i in range(channels):
        who = jnp.int32(0)
        for w in range(channels):
            who = who + jnp.where(places[w] == i, w, 0)
        order_ref[i] = who

    gram_ref[...] = jnp.zeros_like(gram_ref)
    rows_ref[...] = jnp.zeros_like(rows_ref)
    proj_ref[...] = jnp.zeros_like(proj_ref)

    @pl.loop(0, width // CHUNK)
    def _(c):
        at = pl.ds(pl.multiple_of(c * CHUNK, CHUNK), CHUNK)
        pinv_ref[at, :] = 1.0 / precond_ref[at, :]
        for k in range(1, MATVECS):
            basis_ref[k, at, :] = jnp.zeros((CHUNK, width), bf16)

    @pl.loop(0, ROWS // CHUNK)
    def _(c):
        at = pl.ds(pl.multiple_of(c * CHUNK, CHUNK), CHUNK)
        prefix_ref[0, at, :] = jnp.zeros((CHUNK, width), f32)

    @pl.when(sec == 0)
    def _():
        @pl.loop(0, MATVECS * tiles)
        def _(n):
            up_in[n] = jnp.zeros((ROWS, width), bf16)

    @pl.when(sec == secs - 1)
    def _():
        @pl.loop(0, MATVECS * tiles)
        def _(n):
            low_in[n] = jnp.zeros((ROWS, width), bf16)

    def masked(values, start):
        row = start + lax.broadcasted_iota(jnp.int32, values.shape, 0)
        column = lax.broadcasted_iota(jnp.int32, values.shape, 1)
        inside = (row < dims_ref[0]) & (column < dims_ref[1])
        return jnp.where(inside, values, 0.0)

    def sum_copies(r):
        own = slots_ref.at[r, sec]
        return [
            remote(
                own, own, sum_send.at[r], sum_recv.at[r],
                (seg, lax.rem(sec + offset, secs)),
            )
            for offset in range(1, secs)
        ]

    def total(r, tile):
        slots_ref[r, sec] = tile
        for copy in sum_copies(r):
            copy.start()
        arrived = slots_ref.at[r, pl.ds(0, secs - 1)]
        pltpu.make_async_copy(arrived, arrived, sum_recv.at[r]).wait()
        return jnp.sum(slots_ref[r], axis=0) * (1.0 / count)

    send_inv.wait_recv()
    scaled_ref[...] = (
        block_ref[...].astype(f32) * ninv_ref[...].astype(f32)
    ).astype(bf16)
    send_block.wait_recv()

    @pl.loop(0, tiles)
    def _(t):
        at = pl.ds(pl.multiple_of(t * ROWS, ROWS), ROWS)
        image_ref[at, :] = masked(
            jnp.dot(scaled_ref[at, :], nb_ref[...], preferred_element_type=f32), t * ROWS
        )

    def square(c, carry):
        part = image_ref[pl.ds(pl.multiple_of(c * CHUNK, CHUNK), CHUNK), :]
        return carry + fold(part * part)

    guess_sq = lax.fori_loop(0, width // CHUNK, square, jnp.zeros((8, 128), f32))
    guess_sq = jnp.sum(total(0, guess_sq), axis=(0, 1), keepdims=True)
    scale = lax.rsqrt(guess_sq + EPS)

    @pl.loop(0, width // CHUNK)
    def _(c):
        at = pl.ds(pl.multiple_of(c * CHUNK, CHUNK), CHUNK)
        basis_ref[0, at, :] = (image_ref[at, :] * scale).astype(bf16)

    load_left.wait()
    load_right.wait()

    def up_copy(n):
        return remote(
            up_out.at[n], up_in.at[n], halo_send.at[0, n], halo_recv.at[0, n],
            (seg, lax.rem(sec + 1, secs)),
        )

    def low_copy(n):
        return remote(
            low_out.at[n], low_in.at[n], halo_send.at[1, n], halo_recv.at[1, n],
            (seg, lax.rem(sec + secs - 1, secs)),
        )

    @pl.loop(0, MATVECS)
    def _(k):
        def process(t, carry):
            n = k * tiles + t

            @pl.when(sec > 0)
            def _():
                up_copy(n).wait_recv()

            @pl.when(sec < secs - 1)
            def _():
                low_copy(n).wait_recv()

            def body(c, carry):
                inner = pl.ds(pl.multiple_of(c * CHUNK, CHUNK), CHUNK)
                start = t * ROWS + c * CHUNK
                at = pl.ds(pl.multiple_of(start, CHUNK), CHUNK)
                image = stay_ref[at, :] + up_in[n, inner, :].astype(f32)
                image = masked(image + low_in[n, inner, :].astype(f32), start)
                image_ref[at, :] = image
                pinv = pinv_ref[at, :]
                lifted = image * pinv
                new = []
                for j in range(MATVECS):
                    vector = basis_ref[j, at, :].astype(f32)
                    new.append(fold(vector * image))
                    new.append(fold(vector * lifted))
                new.append(fold(lifted * lifted))
                lifted_x = basis_ref[k, at, :].astype(f32) * pinv
                new.append(fold(lifted * lifted_x))
                return tuple(a + b for a, b in zip(carry, new))

            return lax.fori_loop(0, ROWS // CHUNK, body, carry)

        def step(t, carry):
            n = k * tiles + t
            at = pl.ds(pl.multiple_of(t * ROWS, ROWS), ROWS)
            vector = basis_ref[k]
            for w in range(channels):
                lx_ref[w] = jnp.dot(
                    left_ref[w, at, :], vector, preferred_element_type=f32
                ).astype(bf16)
            for i in range(channels):
                w = order_ref[i]
                term = lax.dot_general(
                    lx_ref[w], right_ref[w], (((1,), (1,)), ((), ())),
                    preferred_element_type=f32,
                )
                prefix_ref[i + 1] = prefix_ref[i] + term
            first = prefix_ref[raising]
            second = prefix_ref[moving]
            up_out[n] = first.astype(bf16)
            low_out[n] = (second - first).astype(bf16)

            @pl.when(sec < secs - 1)
            def _():
                up_copy(n).start()

            @pl.when(sec > 0)
            def _():
                low_copy(n).start()

            stay_ref[at, :] = prefix_ref[channels] - second
            return carry

        zeros = tuple(jnp.zeros((8, 128), f32) for _ in range(2 * MATVECS + 2))
        step(0, 0)

        def pipelined(t, carry):
            step(t, 0)
            return process(t - 1, carry)

        carry = lax.fori_loop(1, tiles, pipelined, zeros)

        def own(c, carry):
            at = pl.ds(pl.multiple_of(c * CHUNK, CHUNK), CHUNK)
            current = basis_ref[k, at, :].astype(f32)
            lifted = current * pinv_ref[at, :]
            new = []
            for j in range(MATVECS):
                vector = basis_ref[j, at, :].astype(f32)
                new.append(fold(vector * current))
                new.append(fold(vector * lifted))
            new.append(fold(lifted * lifted))
            return tuple(a + b for a, b in zip(carry, new))

        own_carry = lax.fori_loop(
            0, width // CHUNK, own,
            tuple(jnp.zeros((8, 128), f32) for _ in range(2 * MATVECS + 1)),
        )
        carry = process(tiles - 1, carry)

        def put(row, value):
            rows_ref[row : row + 1, :] = jnp.sum(value, axis=0, keepdims=True)

        for j in range(MATVECS):
            put(j, carry[2 * j])
            put(4 + j, own_carry[2 * j])
            put(8 + j, carry[2 * j + 1])
            put(12 + j, own_carry[2 * j + 1])
        put(16, carry[2 * MATVECS])
        put(17, carry[2 * MATVECS + 1])
        put(18, own_carry[2 * MATVECS])
        sums = jnp.sum(rows_ref[...], axis=1, keepdims=True)
        lane = lax.broadcasted_iota(jnp.int32, (8, 128), 1)
        tile = jnp.where(
            lane == 0, sums[0:8], jnp.where(lane == 1, sums[8:16], sums[16:24])
        )
        tile = total(k + 1, tile)
        gram_ref[k] = tile
        proj_ref[...] = jnp.where(lane == k, tile[:, 0:1], proj_ref[...])

        def entry(source, row, at):
            return source[row : row + 1, at : at + 1]

        row = lax.broadcasted_iota(jnp.int32, (8, 128), 0)
        theta = jnp.sum(
            jnp.where((row == k) & (lane == 0), tile, 0.0), axis=(0, 1), keepdims=True
        )
        weights = [
            entry(tile, j, 1) - theta * entry(tile, 4 + j, 1) for j in range(MATVECS)
        ]
        norm_sq = (
            entry(tile, 0, 2) - 2.0 * theta * entry(tile, 1, 2)
            + theta * theta * entry(tile, 2, 2)
        )
        for i in range(MATVECS):
            column = gram_ref[i]
            inner = weights[i] * entry(column, 4 + i, 0) - 2.0 * weights[i]
            for j in range(i):
                inner = inner + 2.0 * weights[j] * entry(column, 4 + j, 0)
            norm_sq = norm_sq + weights[i] * inner
        scale = lax.rsqrt(jnp.maximum(norm_sq, 0.0) + EPS)

        def update(c, target):
            at = pl.ds(pl.multiple_of(c * CHUNK, CHUNK), CHUNK)
            current = basis_ref[k, at, :].astype(f32)
            remain = (image_ref[at, :] - theta * current) * pinv_ref[at, :]
            for j in range(MATVECS):
                remain = remain - weights[j] * basis_ref[j, at, :].astype(f32)
            target[at, :] = (remain * scale).astype(bf16)

        @pl.loop(0, width // CHUNK)
        def _(c):
            update(c, basis_ref.at[k + 1])

    @pl.loop(0, width // CHUNK)
    def _(c):
        at = pl.ds(pl.multiple_of(c * CHUNK, CHUNK), CHUNK)
        next_ref[at, :] = basis_ref[MATVECS, at, :]

    projected_ref[...] = proj_ref[:MATVECS, :MATVECS]

    send_inv.wait_send()
    send_block.wait_send()

    @pl.when(sec < secs - 1)
    def _():
        @pl.loop(0, MATVECS * tiles)
        def _(n):
            up_copy(n).wait_send()

    @pl.when(sec > 0)
    def _():
        @pl.loop(0, MATVECS * tiles)
        def _(n):
            low_copy(n).wait_send()

    @pl.loop(0, MATVECS + 1)
    def _(r):
        sent = slots_ref.at[r, pl.ds(0, secs - 1)]
        pltpu.make_async_copy(sent, sent, sum_send.at[r]).wait()


def per_device(
    left_env, right_env, left_block, right_block, inv_sv, precond, sector_dims, channel_charge
):
    segs, secs = lax.axis_size("seg"), lax.axis_size("sec")
    channels, width = left_env.shape[2], left_env.shape[-1]
    tiles = width // ROWS
    halos = MATVECS * tiles
    f32, bf16 = jnp.float32, jnp.bfloat16
    vmem = pl.BlockSpec(memory_space=pltpu.VMEM)
    smem = pl.BlockSpec(memory_space=pltpu.SMEM)
    hbm = pl.BlockSpec(memory_space=pl.ANY)
    following, image, projected = pl.pallas_call(
        functools.partial(kernel, segs, secs),
        name="davidson",
        out_shape=(
            jax.ShapeDtypeStruct((width, width), bf16),
            jax.ShapeDtypeStruct((width, width), f32),
            jax.ShapeDtypeStruct((MATVECS, MATVECS), f32),
        ),
        in_specs=[smem, smem, hbm, hbm, vmem, hbm, vmem, vmem],
        out_specs=(vmem, vmem, vmem),
        scratch_shapes=[
            pltpu.VMEM((channels, width, width), bf16),
            pltpu.VMEM((channels, width, width), bf16),
            pltpu.VMEM((width, width), bf16),
            pltpu.VMEM((1, width), bf16),
            pltpu.VMEM((width, width), bf16),
            pltpu.VMEM((width, width), f32),
            pltpu.VMEM((MATVECS + 1, width, width), bf16),
            pltpu.VMEM((channels, ROWS, width), bf16),
            pltpu.VMEM((channels + 1, ROWS, width), f32),
            pltpu.VMEM((width, width), f32),
            pltpu.VMEM((halos, ROWS, width), bf16),
            pltpu.VMEM((halos, ROWS, width), bf16),
            pltpu.VMEM((halos, ROWS, width), bf16),
            pltpu.VMEM((halos, ROWS, width), bf16),
            pltpu.VMEM((MATVECS + 1, secs, 8, 128), f32),
            pltpu.VMEM((24, 128), f32),
            pltpu.VMEM((MATVECS, 8, 128), f32),
            pltpu.VMEM((8, 128), f32),
            pltpu.SMEM((channels,), jnp.int32),
            pltpu.SemaphoreType.DMA((2,)),
            pltpu.SemaphoreType.DMA((2,)),
            pltpu.SemaphoreType.DMA((2,)),
            pltpu.SemaphoreType.DMA((2, halos)),
            pltpu.SemaphoreType.DMA((2, halos)),
            pltpu.SemaphoreType.DMA((MATVECS + 1,)),
            pltpu.SemaphoreType.DMA((MATVECS + 1,)),
        ],
        compiler_params=pltpu.CompilerParams(
            collective_id=0, has_side_effects=True, vmem_limit_bytes=60 * 1024 * 1024
        ),
    )(
        channel_charge, sector_dims[0, 0], left_env[0, 0], right_env[0, 0],
        left_block[0, 0], right_block[0, 0], inv_sv[0], precond[0, 0],
    )
    return following[None, None], image[None, None], projected[None]


def solution(mesh):
    in_specs = (
        P("seg", "sec", None, None, None),
        P("seg", "sec", None, None, None),
        P("seg", "sec", None, None),
        P("seg", "sec", None, None),
        P("seg", "sec", None),
        P("seg", "sec", None, None),
        P("seg", "sec", None),
        P(),
    )
    out_specs = (P("seg", "sec", None, None), P("seg", "sec", None, None), P("seg", None, None))
    return jax.shard_map(
        per_device, mesh=mesh, in_specs=in_specs, out_specs=out_specs, check_vma=False
    )
```

time: 388 us -> 130 us (0.34)
  blocking collectives: 158 us -> 0 us
  Pallas kernels: 0 us -> 123 us
  between operations: 76.6 us -> 0.64 us
  matrix products: 61.3 us -> 0 us
  other arithmetic: 52.6 us -> 0 us
  starting transfers between devices: 17.3 us -> 0 us
  waiting for transfers between devices: 16.5 us -> 0 us
    psum x9 -> x0, blocking collectives: 158 us -> none  [the longest x4 81.1 us: per_device(): lax.psum(tuple((local_dot(basis_float[j], image) for j in range(step + 1)...]
    pallas_call x0 -> x1, Pallas kernels: none -> 123 us  [per_device(): pl.pallas_call(functools.partial(kernel, segs, secs), name='davidson', ou...]
    dot_general x5 -> x0, matrix products: 61.3 us -> none  [the longest x4 59.1 us: per_device(): jnp.einsum('wac,wdc->wad', left_x, renv, preferred_element_type=jnp.float32)]
    reduce_sum x8 -> x0, other arithmetic: 28.9 us -> none  [local_dot(): return jnp.sum(first * second) / count]
    ppermute x10 -> x0, starting transfers between devices: 17.3 us -> none  [the longest x8 12.7 us: shifted_2(): return lax.ppermute(x, axis, pairs)]
    ppermute x10 -> x0, waiting for transfers between devices: 16.5 us -> none  [the longest x8 9.67 us: shifted_2(): return lax.ppermute(x, axis, pairs)]
    convert_element_type x5 -> x0, other arithmetic: 10 us -> none  [the longest x3 9.27 us: per_device(): following = (remain * lax.rsqrt(total_sq + eps)).astype(jnp.bfloat16)]
    another operation x4 -> x0, other arithmetic: 6.56 us -> none  [per_device(): projected = jnp.stack(columns, axis=1)]
  transfers between devices with their start and end apart: 10 -> 0, of which waited for: 8 -> 0; matrix products, arithmetic and copies ran while one was open for 1% -> 0% of each run, Pallas kernels for 0% -> 0%
where the time goes in v1:
time: 130 us; the launch traced here: 129 us
  Pallas kernels  123 us (95%)
  local copies, waits for them, and re-layouts  5.38 us (4%)
    pallas_call x1, Pallas kernels, per_device(): pl.pallas_call(functools.partial(kernel, segs, secs), name='davidson', ou...  123 us
    unnamed x3, local copies, waits for them, and re-layouts  5.38 us

profile of v1, /device:TPU:0, one launch (start us, length us, event | category | flops | bytes accessed | tf_op | source)
XLA Modules:
  0.0 129.5 jit_solution(10900640483110911160)
XLA Ops:
  0.6 123.5 %davidson.1 = (bf16[512,512]{1,0:T(8,128)(2,1)}, f32[512,512]{1,0:T(8,128)}, f32[4,4]{1,0:T(4,128)}) custom-call(s32[13]{0:T(128)} %charge_ref.1, s32[2]{0:T(128)} %bitcast.19, bf16[13,512,512]{2,1,0:T(8,128)(2,1)} %bitcast.10, bf16[13,512,512]{2,1,0:T(8,128)(2,1)} %bitcast.11, bf16[512,512]{1,0:T(8,128)(2,1)} %bitcast.14, bf16[512,512]{1,0:T(8,128)(2,1)} %bitcast.15, ...), custom_call_target="tpu_custom_call" | custom-call | tf_op jit(solution)/shard_map/davidson/pallas_call | solution.py:372
  124.1 1.9 %copy.14 = bf16[1,1,512,512]{3,2,1,0:T(8,128)(2,1)} copy(bf16[1,1,512,512]{3,2,1,0:T(8,128)(2,1)} %bitcast.16) | data formatting | bytes 1048576
  126.0 2.3 %copy.15 = f32[1,1,512,512]{3,2,1,0:T(8,128)} copy(f32[1,1,512,512]{3,2,1,0:T(8,128)} %bitcast.13) | data formatting | bytes 2097152
  128.2 1.2 copy.16

commit v2 on v1

--- a/solution.py
+++ b/solution.py
@@ -9,8 +9,10 @@
 
 MATVECS = 4
 EPS = 1e-06
-ROWS = 128
+ROWS = 256
+COLS = 256
 CHUNK = 32
+BLOCK = 64
 MESH = pl.DeviceIdType.MESH
 
 
@@ -25,14 +27,16 @@
 
 def kernel(
     segs, secs,
-    charge_ref, dims_ref, left_hbm, right_hbm, block_ref, other_hbm, inv_ref, precond_ref,
+    charge_ref, dims_ref, left_hbm, right_hbm, block_hbm, other_hbm, inv_ref, precond_hbm,
     next_ref, image_ref, projected_ref,
-    left_ref, right_ref, nb_ref, ninv_ref, scaled_ref, pinv_ref, basis_ref, lx_ref, prefix_ref,
+    left_ref, right_ref, block_ref, precond_ref, nb_ref, ninv_ref, scaled_ref, pinv_ref, basis_ref, lx_ref, prefix_ref,
     stay_ref, up_out, low_out, up_in, low_in, slots_ref, rows_ref, gram_ref, proj_ref, order_ref,
     load_sem, guess_send, guess_recv, halo_send, halo_recv, sum_send, sum_recv,
 ):
     channels, width, _ = left_ref.shape
     tiles = width // ROWS
+    halves = width // COLS
+    pieces = tiles * halves
     count = secs * width * width
     f32, bf16 = jnp.float32, jnp.bfloat16
     seg, sec = lax.axis_index("seg"), lax.axis_index("sec")
@@ -41,6 +45,10 @@
 
     load_left = pltpu.make_async_copy(left_hbm, left_ref, load_sem.at[0])
     load_right = pltpu.make_async_copy(right_hbm, right_ref, load_sem.at[1])
+    load_block = pltpu.make_async_copy(block_hbm, block_ref, load_sem.at[2])
+    load_precond = pltpu.make_async_copy(precond_hbm, precond_ref, load_sem.at[3])
+    load_precond.start()
+    load_block.start()
     load_left.start()
     load_right.start()
 
@@ -91,6 +99,7 @@
             who = who + jnp.where(places[w] == i, w, 0)
         order_ref[i] = who
 
+    load_precond.wait()
     gram_ref[...] = jnp.zeros_like(gram_ref)
     rows_ref[...] = jnp.zeros_like(rows_ref)
     proj_ref[...] = jnp.zeros_like(proj_ref)
@@ -105,23 +114,23 @@
     @pl.loop(0, ROWS // CHUNK)
     def _(c):
         at = pl.ds(pl.multiple_of(c * CHUNK, CHUNK), CHUNK)
-        prefix_ref[0, at, :] = jnp.zeros((CHUNK, width), f32)
+        prefix_ref[0, at, :] = jnp.zeros((CHUNK, COLS), f32)
 
     @pl.when(sec == 0)
     def _():
-        @pl.loop(0, MATVECS * tiles)
+        @pl.loop(0, MATVECS * pieces)
         def _(n):
-            up_in[n] = jnp.zeros((ROWS, width), bf16)
+            up_in[n] = jnp.zeros((ROWS, COLS), bf16)
 
     @pl.when(sec == secs - 1)
     def _():
-        @pl.loop(0, MATVECS * tiles)
+        @pl.loop(0, MATVECS * pieces)
         def _(n):
-            low_in[n] = jnp.zeros((ROWS, width), bf16)
-
-    def masked(values, start):
+            low_in[n] = jnp.zeros((ROWS, COLS), bf16)
+
+    def masked(values, start, left=0):
         row = start + lax.broadcasted_iota(jnp.int32, values.shape, 0)
-        column = lax.broadcasted_iota(jnp.int32, values.shape, 1)
+        column = left + lax.broadcasted_iota(jnp.int32, values.shape, 1)
         inside = (row < dims_ref[0]) & (column < dims_ref[1])
         return jnp.where(inside, values, 0.0)
 
@@ -144,6 +153,7 @@
         return jnp.sum(slots_ref[r], axis=0) * (1.0 / count)
 
     send_inv.wait_recv()
+    load_block.wait()
     scaled_ref[...] = (
         block_ref[...].astype(f32) * ninv_ref[...].astype(f32)
     ).astype(bf16)
@@ -161,13 +171,12 @@
         return carry + fold(part * part)
 
     guess_sq = lax.fori_loop(0, width // CHUNK, square, jnp.zeros((8, 128), f32))
-    guess_sq = jnp.sum(total(0, guess_sq), axis=(0, 1), keepdims=True)
-    scale = lax.rsqrt(guess_sq + EPS)
+    rows_ref[19:20, :] = jnp.sum(guess_sq, axis=0, keepdims=True)
 
     @pl.loop(0, width // CHUNK)
     def _(c):
         at = pl.ds(pl.multiple_of(c * CHUNK, CHUNK), CHUNK)
-        basis_ref[0, at, :] = (image_ref[at, :] * scale).astype(bf16)
+        basis_ref[0, at, :] = image_ref[at, :].astype(bf16)
 
     load_left.wait()
     load_right.wait()
@@ -186,8 +195,10 @@
 
     @pl.loop(0, MATVECS)
     def _(k):
-        def process(t, carry):
-            n = k * tiles + t
+        def process(piece, carry):
+            t, h = divmod(piece, halves)
+            n = k * pieces + piece
+            across = pl.ds(h * COLS, COLS)
 
             @pl.when(sec > 0)
             def _():
@@ -198,65 +209,57 @@
                 low_copy(n).wait_recv()
 
             def body(c, carry):
-                inner = pl.ds(pl.multiple_of(c * CHUNK, CHUNK), CHUNK)
-                start = t * ROWS + c * CHUNK
-                at = pl.ds(pl.multiple_of(start, CHUNK), CHUNK)
-                image = stay_ref[at, :] + up_in[n, inner, :].astype(f32)
-                image = masked(image + low_in[n, inner, :].astype(f32), start)
-                image_ref[at, :] = image
-                pinv = pinv_ref[at, :]
+                inner = pl.ds(pl.multiple_of(c * BLOCK, BLOCK), BLOCK)
+                start = t * ROWS + c * BLOCK
+                at = pl.ds(pl.multiple_of(start, BLOCK), BLOCK)
+                image = stay_ref[at, across] + up_in[n, inner, :].astype(f32)
+                image = masked(image + low_in[n, inner, :].astype(f32), start, h * COLS)
+                image_ref[at, across] = image
+                pinv = pinv_ref[at, across]
                 lifted = image * pinv
                 new = []
                 for j in range(MATVECS):
-                    vector = basis_ref[j, at, :].astype(f32)
+                    vector = basis_ref[j, at, across].astype(f32)
                     new.append(fold(vector * image))
                     new.append(fold(vector * lifted))
                 new.append(fold(lifted * lifted))
-                lifted_x = basis_ref[k, at, :].astype(f32) * pinv
+                lifted_x = basis_ref[k, at, across].astype(f32) * pinv
                 new.append(fold(lifted * lifted_x))
                 return tuple(a + b for a, b in zip(carry, new))
 
-            return lax.fori_loop(0, ROWS // CHUNK, body, carry)
-
-        def step(t, carry):
-            n = k * tiles + t
-            at = pl.ds(pl.multiple_of(t * ROWS, ROWS), ROWS)
+            return lax.fori_loop(0, ROWS // BLOCK, body, carry)
+
+        for t in range(tiles):
+            rows = pl.ds(t * ROWS, ROWS)
             vector = basis_ref[k]
             for w in range(channels):
                 lx_ref[w] = jnp.dot(
-                    left_ref[w, at, :], vector, preferred_element_type=f32
+                    left_ref[w, rows, :], vector, preferred_element_type=f32
                 ).astype(bf16)
-            for i in range(channels):
-                w = order_ref[i]
-                term = lax.dot_general(
-                    lx_ref[w], right_ref[w], (((1,), (1,)), ((), ())),
-                    preferred_element_type=f32,
-                )
-                prefix_ref[i + 1] = prefix_ref[i] + term
-            first = prefix_ref[raising]
-            second = prefix_ref[moving]
-            up_out[n] = first.astype(bf16)
-            low_out[n] = (second - first).astype(bf16)
-
-            @pl.when(sec < secs - 1)
-            def _():
-                up_copy(n).start()
-
-            @pl.when(sec > 0)
-            def _():
-                low_copy(n).start()
-
-            stay_ref[at, :] = prefix_ref[channels] - second
-            return carry
-
-        zeros = tuple(jnp.zeros((8, 128), f32) for _ in range(2 * MATVECS + 2))
-        step(0, 0)
-
-        def pipelined(t, carry):
-            step(t, 0)
-            return process(t - 1, carry)
-
-        carry = lax.fori_loop(1, tiles, pipelined, zeros)
+            for h in range(halves):
+                n = k * pieces + t * halves + h
+                across = pl.ds(h * COLS, COLS)
+                for i in range(channels):
+                    w = order_ref[i]
+                    term = lax.dot_general(
+                        lx_ref[w], right_ref[w, across, :], (((1,), (1,)), ((), ())),
+                        preferred_element_type=f32,
+                    )
+                    prefix_ref[i + 1] = prefix_ref[i] + term
+                first = prefix_ref[raising]
+                second = prefix_ref[moving]
+                up_out[n] = first.astype(bf16)
+                low_out[n] = (second - first).astype(bf16)
+
+                @pl.when(sec < secs - 1)
+                def _():
+                    up_copy(n).start()
+
+                @pl.when(sec > 0)
+                def _():
+                    low_copy(n).start()
+
+                stay_ref[rows, across] = prefix_ref[channels] - second
 
         def own(c, carry):
             at = pl.ds(pl.multiple_of(c * CHUNK, CHUNK), CHUNK)
@@ -274,7 +277,9 @@
             0, width // CHUNK, own,
             tuple(jnp.zeros((8, 128), f32) for _ in range(2 * MATVECS + 1)),
         )
-        carry = process(tiles - 1, carry)
+        carry = tuple(jnp.zeros((8, 128), f32) for _ in range(2 * MATVECS + 2))
+        for piece in range(pieces):
+            carry = process(piece, carry)
 
         def put(row, value):
             rows_ref[row : row + 1, :] = jnp.sum(value, axis=0, keepdims=True)
@@ -292,12 +297,16 @@
         tile = jnp.where(
             lane == 0, sums[0:8], jnp.where(lane == 1, sums[8:16], sums[16:24])
         )
-        tile = total(k + 1, tile)
+        tile = total(k, tile)
+
+        def entry(source, row, at):
+            return source[row : row + 1, at : at + 1]
+
+        guess_scale = lax.rsqrt(entry(tile, 3, 2) + EPS)
+        factor = jnp.where(k == 0, guess_scale, 1.0)
+        tile = tile * (factor * factor)
         gram_ref[k] = tile
         proj_ref[...] = jnp.where(lane == k, tile[:, 0:1], proj_ref[...])
-
-        def entry(source, row, at):
-            return source[row : row + 1, at : at + 1]
 
         row = lax.broadcasted_iota(jnp.int32, (8, 128), 0)
         theta = jnp.sum(
@@ -318,10 +327,17 @@
             norm_sq = norm_sq + weights[i] * inner
         scale = lax.rsqrt(jnp.maximum(norm_sq, 0.0) + EPS)
 
+        @pl.when(k == 0)
+        def _():
+            @pl.loop(0, width // CHUNK)
+            def _(c):
+                at = pl.ds(pl.multiple_of(c * CHUNK, CHUNK), CHUNK)
+                basis_ref[0, at, :] = (basis_ref[0, at, :].astype(f32) * guess_scale).astype(bf16)
+
         def update(c, target):
             at = pl.ds(pl.multiple_of(c * CHUNK, CHUNK), CHUNK)
             current = basis_ref[k, at, :].astype(f32)
-            remain = (image_ref[at, :] - theta * current) * pinv_ref[at, :]
+            remain = (image_ref[at, :] * factor - theta * current) * pinv_ref[at, :]
             for j in range(MATVECS):
                 remain = remain - weights[j] * basis_ref[j, at, :].astype(f32)
             target[at, :] = (remain * scale).astype(bf16)
@@ -342,20 +358,26 @@
 
     @pl.when(sec < secs - 1)
     def _():
-        @pl.loop(0, MATVECS * tiles)
+        @pl.loop(0, MATVECS * pieces)
         def _(n):
             up_copy(n).wait_send()
 
     @pl.when(sec > 0)
     def _():
-        @pl.loop(0, MATVECS * tiles)
+        @pl.loop(0, MATVECS * pieces)
         def _(n):
             low_copy(n).wait_send()
 
-    @pl.loop(0, MATVECS + 1)
+    @pl.loop(0, MATVECS)
     def _(r):
         sent = slots_ref.at[r, pl.ds(0, secs - 1)]
         pltpu.make_async_copy(sent, sent, sum_send.at[r]).wait()
+
+
+def finish(next_in, image_in, projected_in, next_ref, image_ref, projected_ref):
+    next_ref[...] = next_in[...]
+    image_ref[...] = image_in[...]
+    projected_ref[...] = projected_in[...]
 
 
 def per_device(
@@ -363,49 +385,51 @@
 ):
     segs, secs = lax.axis_size("seg"), lax.axis_size("sec")
     channels, width = left_env.shape[2], left_env.shape[-1]
-    tiles = width // ROWS
-    halos = MATVECS * tiles
+    halos = MATVECS * (width // ROWS) * (width // COLS)
     f32, bf16 = jnp.float32, jnp.bfloat16
     vmem = pl.BlockSpec(memory_space=pltpu.VMEM)
     smem = pl.BlockSpec(memory_space=pltpu.SMEM)
     hbm = pl.BlockSpec(memory_space=pl.ANY)
-    following, image, projected = pl.pallas_call(
+    out_shape = (
+        jax.ShapeDtypeStruct((width, width), bf16),
+        jax.ShapeDtypeStruct((width, width), f32),
+        jax.ShapeDtypeStruct((MATVECS, MATVECS), f32),
+    )
+    results = pl.pallas_call(
         functools.partial(kernel, segs, secs),
         name="davidson",
-        out_shape=(
-            jax.ShapeDtypeStruct((width, width), bf16),
-            jax.ShapeDtypeStruct((width, width), f32),
-            jax.ShapeDtypeStruct((MATVECS, MATVECS), f32),
-        ),
-        in_specs=[smem, smem, hbm, hbm, vmem, hbm, vmem, vmem],
+        out_shape=out_shape,
+        in_specs=[smem, smem, hbm, hbm, hbm, hbm, vmem, hbm],
         out_specs=(vmem, vmem, vmem),
         scratch_shapes=[
             pltpu.VMEM((channels, width, width), bf16),
             pltpu.VMEM((channels, width, width), bf16),
+            pltpu.VMEM((width, width), bf16),
+            pltpu.VMEM((width, width), f32),
             pltpu.VMEM((width, width), bf16),
             pltpu.VMEM((1, width), bf16),
             pltpu.VMEM((width, width), bf16),
             pltpu.VMEM((width, width), f32),
             pltpu.VMEM((MATVECS + 1, width, width), bf16),
             pltpu.VMEM((channels, ROWS, width), bf16),
-            pltpu.VMEM((channels + 1, ROWS, width), f32),
+            pltpu.VMEM((channels + 1, ROWS, COLS), f32),
             pltpu.VMEM((width, width), f32),
-            pltpu.VMEM((halos, ROWS, width), bf16),
-            pltpu.VMEM((halos, ROWS, width), bf16),
-            pltpu.VMEM((halos, ROWS, width), bf16),
-            pltpu.VMEM((halos, ROWS, width), bf16),
-            pltpu.VMEM((MATVECS + 1, secs, 8, 128), f32),
+            pltpu.VMEM((halos, ROWS, COLS), bf16),
+            pltpu.VMEM((halos, ROWS, COLS), bf16),
+            pltpu.VMEM((halos, ROWS, COLS), bf16),
+            pltpu.VMEM((halos, ROWS, COLS), bf16),
+            pltpu.VMEM((MATVECS, secs, 8, 128), f32),
             pltpu.VMEM((24, 128), f32),
             pltpu.VMEM((MATVECS, 8, 128), f32),
             pltpu.VMEM((8, 128), f32),
             pltpu.SMEM((channels,), jnp.int32),
-            pltpu.SemaphoreType.DMA((2,)),
+            pltpu.SemaphoreType.DMA((4,)),
             pltpu.SemaphoreType.DMA((2,)),
             pltpu.SemaphoreType.DMA((2,)),
             pltpu.SemaphoreType.DMA((2, halos)),
             pltpu.SemaphoreType.DMA((2, halos)),
-            pltpu.SemaphoreType.DMA((MATVECS + 1,)),
-            pltpu.SemaphoreType.DMA((MATVECS + 1,)),
+            pltpu.SemaphoreType.DMA((MATVECS,)),
+            pltpu.SemaphoreType.DMA((MATVECS,)),
         ],
         compiler_params=pltpu.CompilerParams(
             collective_id=0, has_side_effects=True, vmem_limit_bytes=60 * 1024 * 1024
@@ -414,6 +438,10 @@
         channel_charge, sector_dims[0, 0], left_env[0, 0], right_env[0, 0],
         left_block[0, 0], right_block[0, 0], inv_sv[0], precond[0, 0],
     )
+    following, image, projected = pl.pallas_call(
+        finish, name="finish", out_shape=out_shape,
+        in_specs=[vmem] * 3, out_specs=(vmem, vmem, vmem),
+    )(*results)
     return following[None, None], image[None, None], projected[None]
 
 

time: 130 us -> 101 us (0.78)
  Pallas kernels: 123 us -> 100 us
  local copies, waits for them, and re-layouts: 5.38 us -> 0 us
    pallas_call x1, Pallas kernels: 123 us -> 97.7 us  [per_device(): pl.pallas_call(functools.partial(kernel, segs, secs), name='davidson', ou...]
    unnamed x3 -> x0, local copies, waits for them, and re-layouts: 5.38 us -> none
    pallas_call x0 -> x1, Pallas kernels: none -> 2.57 us  [per_device(): pl.pallas_call(finish, name='finish', out_shape=out_shape, in_specs=[vmem...]
where the time goes in v2:
time: 101 us
  Pallas kernels  100 us (99%)
    pallas_call x1, Pallas kernels, per_device(): pl.pallas_call(functools.partial(kernel, segs, secs), name='davidson', ou...  97.7 us
    pallas_call x1, Pallas kernels, per_device(): pl.pallas_call(finish, name='finish', out_shape=out_shape, in_specs=[vmem...  2.57 us

profile of v2, /device:TPU:0, one launch (start us, length us, event | category | flops | bytes accessed | tf_op | source)
XLA Modules:
  0.0 100.9 jit_solution(17501057134097490453)
XLA Ops:
  0.6 97.7 %davidson.1 = (bf16[512,512]{1,0:T(8,128)(2,1)}, f32[512,512]{1,0:T(8,128)}, f32[4,4]{1,0:T(4,128)}) custom-call(s32[13]{0:T(128)} %charge_ref.1, s32[2]{0:T(128)} %bitcast.16, bf16[13,512,512]{2,1,0:T(8,128)(2,1)} %bitcast.10, bf16[13,512,512]{2,1,0:T(8,128)(2,1)} %bitcast.11, bf16[512,512]{1,0:T(8,128)(2,1)} %bitcast.13, bf16[512,512]{1,0:T(8,128)(2,1)} %bitcast.14, ...), custom_call_target="tpu_custom_call" | custom-call | tf_op jit(solution)/shard_map/davidson/pallas_call | solution.py:398
  98.3 2.6 %finish.1 = (bf16[512,512]{1,0:T(8,128)(2,1)}, f32[512,512]{1,0:T(8,128)}, f32[4,4]{1,0:T(4,128)}) custom-call(bf16[512,512]{1,0:T(8,128)(2,1)} %get-tuple-element.9.next_in, f32[512,512]{1,0:T(8,128)} %get-tuple-element.10.image_in, f32[4,4]{1,0:T(4,128)} %get-tuple-element.11.projected_in), custom_call_target="tpu_custom_call" | custom-call | tf_op jit(solution)/shard_map/finish/pallas_call | solution.py:441

commit v3 on v2

--- a/solution.py
+++ b/solution.py
@@ -195,7 +195,7 @@
 
     @pl.loop(0, MATVECS)
     def _(k):
-        def process(piece, carry):
+        def process(kk, piece, carry):
             t, h = divmod(piece, halves)
             n = k * pieces + piece
             across = pl.ds(h * COLS, COLS)
@@ -218,7 +218,7 @@
                 pinv = pinv_ref[at, across]
                 lifted = image * pinv
                 new = []
-                for j in range(MATVECS):
+                for j in range(kk + 1):
                     vector = basis_ref[j, at, across].astype(f32)
                     new.append(fold(vector * image))
                     new.append(fold(vector * lifted))
@@ -261,37 +261,39 @@
 
                 stay_ref[rows, across] = prefix_ref[channels] - second
 
-        def own(c, carry):
-            at = pl.ds(pl.multiple_of(c * CHUNK, CHUNK), CHUNK)
-            current = basis_ref[k, at, :].astype(f32)
-            lifted = current * pinv_ref[at, :]
-            new = []
-            for j in range(MATVECS):
-                vector = basis_ref[j, at, :].astype(f32)
-                new.append(fold(vector * current))
-                new.append(fold(vector * lifted))
-            new.append(fold(lifted * lifted))
-            return tuple(a + b for a, b in zip(carry, new))
-
-        own_carry = lax.fori_loop(
-            0, width // CHUNK, own,
-            tuple(jnp.zeros((8, 128), f32) for _ in range(2 * MATVECS + 1)),
-        )
-        carry = tuple(jnp.zeros((8, 128), f32) for _ in range(2 * MATVECS + 2))
-        for piece in range(pieces):
-            carry = process(piece, carry)
-
         def put(row, value):
             rows_ref[row : row + 1, :] = jnp.sum(value, axis=0, keepdims=True)
 
-        for j in range(MATVECS):
-            put(j, carry[2 * j])
-            put(4 + j, own_carry[2 * j])
-            put(8 + j, carry[2 * j + 1])
-            put(12 + j, own_carry[2 * j + 1])
-        put(16, carry[2 * MATVECS])
-        put(17, carry[2 * MATVECS + 1])
-        put(18, own_carry[2 * MATVECS])
+        def reduce(kk):
+            def own(c, carry):
+                at = pl.ds(pl.multiple_of(c * CHUNK, CHUNK), CHUNK)
+                current = basis_ref[kk, at, :].astype(f32)
+                lifted = current * pinv_ref[at, :]
+                new = []
+                for j in range(kk + 1):
+                    vector = basis_ref[j, at, :].astype(f32)
+                    new.append(fold(vector * current))
+                    new.append(fold(vector * lifted))
+                new.append(fold(lifted * lifted))
+                return tuple(a + b for a, b in zip(carry, new))
+
+            zero = jnp.zeros((8, 128), f32)
+            own_carry = lax.fori_loop(0, width // CHUNK, own, (zero,) * (2 * kk + 3))
+            carry = (zero,) * (2 * kk + 4)
+            for piece in range(pieces):
+                carry = process(kk, piece, carry)
+            for j in range(kk + 1):
+                put(j, carry[2 * j])
+                put(4 + j, own_carry[2 * j])
+                put(8 + j, carry[2 * j + 1])
+                put(12 + j, own_carry[2 * j + 1])
+            put(16, carry[2 * kk + 2])
+            put(17, carry[2 * kk + 3])
+            put(18, own_carry[2 * kk + 2])
+
+        for kk in range(MATVECS):
+            pl.when(k == kk)(functools.partial(reduce, kk))
+
         sums = jnp.sum(rows_ref[...], axis=1, keepdims=True)
         lane = lax.broadcasted_iota(jnp.int32, (8, 128), 1)
         tile = jnp.where(
@@ -334,17 +336,21 @@
                 at = pl.ds(pl.multiple_of(c * CHUNK, CHUNK), CHUNK)
                 basis_ref[0, at, :] = (basis_ref[0, at, :].astype(f32) * guess_scale).astype(bf16)
 
-        def update(c, target):
-            at = pl.ds(pl.multiple_of(c * CHUNK, CHUNK), CHUNK)
-            current = basis_ref[k, at, :].astype(f32)
-            remain = (image_ref[at, :] * factor - theta * current) * pinv_ref[at, :]
-            for j in range(MATVECS):
-                remain = remain - weights[j] * basis_ref[j, at, :].astype(f32)
-            target[at, :] = (remain * scale).astype(bf16)
-
-        @pl.loop(0, width // CHUNK)
-        def _(c):
-            update(c, basis_ref.at[k + 1])
+        def update(kk):
+            @pl.loop(0, width // CHUNK)
+            def _(c):
+                at = pl.ds(pl.multiple_of(c * CHUNK, CHUNK), CHUNK)
+                image = image_ref[at, :]
+                if kk == 0:
+                    image = image * factor
+                current = basis_ref[kk, at, :].astype(f32)
+                remain = (image - theta * current) * pinv_ref[at, :]
+                for j in range(kk + 1):
+                    remain = remain - weights[j] * basis_ref[j, at, :].astype(f32)
+                basis_ref[kk + 1, at, :] = (remain * scale).astype(bf16)
+
+        for kk in range(MATVECS):
+            pl.when(k == kk)(functools.partial(update, kk))
 
     @pl.loop(0, width // CHUNK)
     def _(c):

time: 101 us -> 100 us (0.990)
  no operation moved by 1% of the time
where the time goes in v3:
time: 100 us; the launch traced here: 99.9 us
  Pallas kernels  99.3 us (99%)
    pallas_call x1, Pallas kernels, per_device(): pl.pallas_call(functools.partial(kernel, segs, secs), name='davidson', ou...  96.7 us
    pallas_call x1, Pallas kernels, per_device(): pl.pallas_call(finish, name='finish', out_shape=out_shape, in_specs=[vmem...  2.57 us

profile of v3, /device:TPU:0, one launch (start us, length us, event | category | flops | bytes accessed | tf_op | source)
XLA Modules:
  0.0 99.9 jit_solution(5886619679143824239)
XLA Ops:
  0.6 96.7 %davidson.1 = (bf16[512,512]{1,0:T(8,128)(2,1)}, f32[512,512]{1,0:T(8,128)}, f32[4,4]{1,0:T(4,128)}) custom-call(s32[13]{0:T(128)} %charge_ref.1, s32[2]{0:T(128)} %bitcast.16, bf16[13,512,512]{2,1,0:T(8,128)(2,1)} %bitcast.10, bf16[13,512,512]{2,1,0:T(8,128)(2,1)} %bitcast.11, bf16[512,512]{1,0:T(8,128)(2,1)} %bitcast.13, bf16[512,512]{1,0:T(8,128)(2,1)} %bitcast.14, ...), custom_call_target="tpu_custom_call" | custom-call | tf_op jit(solution)/shard_map/davidson/pallas_call | solution.py:404
  97.3 2.6 %finish.1 = (bf16[512,512]{1,0:T(8,128)(2,1)}, f32[512,512]{1,0:T(8,128)}, f32[4,4]{1,0:T(4,128)}) custom-call(bf16[512,512]{1,0:T(8,128)(2,1)} %get-tuple-element.9.next_in, f32[512,512]{1,0:T(8,128)} %get-tuple-element.10.image_in, f32[4,4]{1,0:T(4,128)} %get-tuple-element.11.projected_in), custom_call_target="tpu_custom_call" | custom-call | tf_op jit(solution)/shard_map/finish/pallas_call | solution.py:447
